TPU v7x, 32 devices: a whole 2x2x4 slice. The times are simulated.
32 devices in a mesh: shard: 4 (over y, x), mp: 4 (over z), segment: 2 (over core).
Axes of the slice: x: 2, y: 2, z: 4, core: 2. Of those that a mesh axis runs over, the one named last changes fastest.
Arguments:
- store_tokens: int32 [256, 48], P('shard'), may hold values from 0 to 16383
- retrieved: int32 [4, 12], replicated, may hold values from 0 to 63
- owner_shard: int32 [48, 1], replicated, may hold values from 0 to 3; in each aligned block of 12 rows (0 to 11, 12 to 23, ...) at most 3 rows name the same one
- targets: int32 [4, 64], P('shard'), may hold values from 0 to 16383
- vocab_table: bfloat16 [16384, 4096], P(None, ('mp', 'segment')), may hold values from -6 to 6
- norm_gains: float32 [3, 4096], replicated, may hold values from 0.1 to 1.9
- layer_weights: bfloat16 [2, 4, 4096, 4096], P('segment', None, 'shard', 'mp'), may hold values from -0.09375 to 0.09375
Outputs:
- encoded: bfloat16 [2304, 4096], P('shard', ('mp', 'segment'))
- decoded: bfloat16 [256, 4096], P('shard', ('mp', 'segment'))
Inputs may be any that keep to these rules, and one draw needn't show every extreme that they name: `owner_shard`: within the 12 passages of one question no shard owns more than 3; in every draw some question has exactly 3 passages from one shard.
All inputs are finite; a program needn't handle non-finite values.
Results may differ from a plain program's by a relative error of at most 0.015.
Values may be sent and summed in bfloat16 or wider, within the bound.
A program may use at most 128 MiB of HBM per device.

v0:
```python
import jax
import jax.numpy as jnp
from jax import lax
from jax.sharding import PartitionSpec as P

D = 4096
DH = 64
epsilon = 1e-06


def attend(query_rows, key_rows, value_rows, head_count):
    batch_size = query_rows.shape[0]
    head_size = query_rows.shape[2] // head_count
    query_heads = query_rows.reshape(batch_size, query_rows.shape[1], head_count, head_size)
    key_heads = key_rows.reshape(batch_size, key_rows.shape[1], head_count, head_size)
    value_heads = value_rows.reshape(batch_size, value_rows.shape[1], head_count, head_size)
    scores = jnp.einsum(
        "brhd,bshd->bhrs", query_heads, key_heads, preferred_element_type=jnp.float32
    ) * head_size ** (-0.5)
    shifted = jnp.exp(scores - jnp.max(scores, axis=-1, keepdims=True))
    attention = (shifted / jnp.sum(shifted, axis=-1, keepdims=True)).astype(jnp.bfloat16)
    mixture = jnp.einsum(
        "bhrs,bshd->brhd", attention, value_heads, preferred_element_type=jnp.float32
    )
    return mixture.astype(jnp.bfloat16).reshape(
        batch_size * query_rows.shape[1], head_count * head_size
    )


def after(value, *others):
    return lax.optimization_barrier((value,) + others)[0]


def swap_segments(weights, first, count):
    me = lax.axis_index("segment")
    rows, half = (weights.shape[2], weights.shape[3] // 2)
    size = (1, count, rows, half)
    kept = lax.dynamic_slice(weights, (0, first, 0, me * half), size)[0]
    sent = lax.dynamic_slice(weights, (0, first, 0, (1 - me) * half), size)[0]
    other = lax.ppermute(sent, "segment", [(0, 1), (1, 0)])
    encoder = jnp.where(me == 0, kept, other)

    def decoder(*others):
        late_kept, late_other = lax.optimization_barrier((kept, other) + others)[:2]
        return jnp.where(me == 0, late_other, late_kept)

    return (encoder, decoder)


X_PAIRS = [(i, i ^ 1) for i in range(4)]
Y_PAIRS = [(i, i ^ 2) for i in range(4)]


def near(block):
    count = lax.axis_size("shard")
    me = lax.axis_index("shard")
    rows = block.shape[1]
    if count != 4:
        whole = lax.all_gather(block, "shard", axis=1, tiled=True)
        return [(i, 0, whole[:, i * rows : (i + 1) * rows]) for i in range(count)]
    return [
        (me, 0, block),
        (me ^ 1, 0, lax.ppermute(block, "shard", X_PAIRS)),
        (me ^ 2, 0, lax.ppermute(block, "shard", Y_PAIRS)),
    ]


def far(pieces):
    if lax.axis_size("shard") != 4:
        return []
    me = lax.axis_index("shard")
    rows = pieces[0][2].shape[1]
    top = lax.ppermute(pieces[2][2][:, : rows // 2], "shard", X_PAIRS)
    bottom = lax.ppermute(pieces[1][2][:, rows // 2 :], "shard", Y_PAIRS)
    return [(me ^ 3, 0, top), (me ^ 3, rows // 2, bottom)]


def blocks(pieces):
    return [piece[2] for piece in pieces]


def project(rows_in, pieces, shard_rows, total=None):
    for owner, first, block in pieces:
        depth = block.shape[1]
        part = lax.dynamic_slice_in_dim(rows_in, owner * shard_rows + first, depth, axis=1)
        term = jnp.einsum("rn,knh->rkh", part, block, preferred_element_type=jnp.float32)
        total = term if total is None else total + term
    return total


def in_order(pieces, shard_rows):
    columns = pieces[0][2].shape[2]
    whole = jnp.zeros((D, columns), jnp.bfloat16)
    for owner, first, block in pieces:
        whole = lax.dynamic_update_slice_in_dim(whole, block[0], owner * shard_rows + first, axis=0)
    return whole


def body(store_tokens, retrieved, owner_shard, targets, vocab_table, norm_gains, layer_weights):
    shard_count = lax.axis_size("shard")
    my_shard = lax.axis_index("shard")
    enc_qkv, dec_qkv = swap_segments(layer_weights, 0, 3)
    per_question = retrieved.shape[1]
    length = store_tokens.shape[1]
    slot_cap = max(2, (per_question + shard_count - 1) // shard_count)
    owners = owner_shard.reshape(retrieved.shape)
    positions = jnp.arange(per_question)
    before = positions[None, :] < positions[:, None]
    matches = owners[:, :, None] == owners[:, None, :]
    slot_rank = jnp.sum(jnp.where(matches & before[None], 1, 0), axis=2).astype(jnp.int32)
    slot_numbers = jnp.arange(slot_cap)
    chosen = (owners[:, None, :] == my_shard) & (
        slot_rank[:, None, :] == slot_numbers[None, :, None]
    )
    local_rows = jnp.sum(jnp.where(chosen, retrieved[:, None, :], 0), axis=2)
    send_ids = jnp.take(store_tokens, local_rows.reshape(-1), axis=0).reshape(
        shard_count, slot_cap, length
    )
    arrived = lax.all_to_all(send_ids, "shard", split_axis=0, concat_axis=0, tiled=True)
    mine_owner = lax.dynamic_index_in_dim(owners, my_shard, 0, keepdims=False)
    mine_rank = lax.dynamic_index_in_dim(slot_rank, my_shard, 0, keepdims=False)
    arrived_rows = arrived.reshape(shard_count * slot_cap, length)
    passage_ids = jnp.take(arrived_rows, mine_owner * slot_cap + mine_rank, axis=0).reshape(-1)
    enc_out, dec_out = swap_segments(layer_weights, 3, 1)
    shard_rows = layer_weights.shape[2]
    head_block = enc_qkv.shape[2]
    head_count = head_block // DH
    pass_rows = passage_ids.shape[0]
    all_ids = after(jnp.concatenate([passage_ids, targets.reshape(-1)]), enc_qkv)
    embedded_part = jnp.take(vocab_table, all_ids, axis=0)
    piece = lax.all_gather(embedded_part, ("mp", "segment"), axis=1, tiled=True)
    passage_part = embedded_part[:pass_rows]
    target_part = embedded_part[pass_rows:]
    rows_f32 = piece.astype(jnp.float32)
    scale = lax.rsqrt(jnp.sum(rows_f32 * rows_f32, axis=1) / D + epsilon)
    pass_normed = (rows_f32[:pass_rows] * norm_gains[0]).astype(jnp.bfloat16)
    targ_normed = (rows_f32[pass_rows:] * norm_gains[1]).astype(jnp.bfloat16)
    enc_near = near(enc_qkv)
    accum = project(pass_normed, enc_near, shard_rows)
    enc_far = far(enc_near)
    out_near = near(after(enc_out, accum))
    accum = project(pass_normed, enc_far, shard_rows, accum)
    cross_near = near(dec_qkv(*blocks(out_near))[1:3])
    out_far = far(out_near)
    projected = (accum * scale[:pass_rows, None, None]).astype(jnp.bfloat16)
    shaped = projected.reshape(per_question, length, 3, head_block)
    context = attend(shaped[:, :, 0], shaped[:, :, 1], shaped[:, :, 2], head_count)
    enc_partial = lax.dot_general(
        context,
        in_order(out_near + out_far, shard_rows),
        (((1,), (1,)), ((), ())),
        preferred_element_type=jnp.float32,
    ).astype(jnp.bfloat16)
    enc_sum = lax.psum_scatter(
        enc_partial, ("mp", "segment"), scatter_dimension=1, tiled=True
    ).astype(jnp.float32)
    query_rows = lax.all_to_all(
        after(targ_normed, enc_partial), "shard", split_axis=1, concat_axis=0, tiled=True
    )
    query_terms = jnp.dot(query_rows, dec_qkv(enc_partial)[0], preferred_element_type=jnp.float32)
    query_terms = lax.all_to_all(query_terms, "shard", split_axis=0, concat_axis=0, tiled=True)
    targ_accum = jnp.sum(query_terms.reshape(shard_count, -1, head_block), axis=0)
    queries = (targ_accum * scale[pass_rows:, None]).astype(jnp.bfloat16)[None]
    enc_sum = after(enc_sum, queries, *blocks(cross_near))
    encoded = (passage_part.astype(jnp.float32) + enc_sum).astype(jnp.bfloat16)
    whole_encoded = lax.all_gather(encoded, ("mp", "segment"), axis=1, tiled=True)
    cross_far = far(cross_near)
    late_near = near(dec_out(*blocks(cross_far), queries))
    whole_encoded = after(whole_encoded, *blocks(cross_far))
    enc_f32 = whole_encoded.astype(jnp.float32)
    enc_scale = lax.rsqrt(jnp.sum(enc_f32 * enc_f32, axis=1) / D + epsilon)
    enc_normed = (enc_f32 * norm_gains[2]).astype(jnp.bfloat16)
    cross_accum = project(enc_normed, cross_near + cross_far, shard_rows)
    late_far = far([(o, f, after(b, cross_accum)) for o, f, b in late_near])
    key_values = (cross_accum * enc_scale[:, None, None]).astype(jnp.bfloat16)
    dec_context = attend(queries, key_values[None, :, 0], key_values[None, :, 1], head_count)
    dec_partial = lax.dot_general(
        dec_context,
        in_order(late_near + late_far, shard_rows),
        (((1,), (1,)), ((), ())),
        preferred_element_type=jnp.float32,
    ).astype(jnp.bfloat16)
    terms = lax.all_to_all(dec_partial, ("mp", "segment"), split_axis=1, concat_axis=0, tiled=True)
    terms = terms.reshape(-1, target_part.shape[0], target_part.shape[1]).astype(jnp.float32)
    decoded = (target_part.astype(jnp.float32) + jnp.sum(terms, axis=0)).astype(jnp.bfloat16)
    return (encoded, decoded)


def solution(mesh):
    placed = (
        P("shard", None),
        P(),
        P(),
        P("shard", None),
        P(None, ("mp", "segment")),
        P(),
        P("segment", None, "shard", "mp"),
    )
    return jax.shard_map(
        body,
        mesh=mesh,
        in_specs=placed,
        out_specs=(P("shard", ("mp", "segment")), P("shard", ("mp", "segment"))),
        check_vma=False,
    )
```

profile of v0, /device:TPU:0, one launch (start us, length us, event | category | flops | bytes accessed | tf_op | source)
XLA Modules:
  0.0 385.7 jit_solution(14812456501296723791)
XLA Ops:
  7.2 3.8 dynamic-slice_bitcast_fusion
  15.2 4.7 %all-to-all-start = ((s32[4,1,144]{2,1,0:T(1,128)}), s32[4,1,144]{2,1,0:T(1,128)S(1)}, u32[]{:S(2)}, u32[]{:S(2)}) async-start(s32[4,1,144]{2,1,0:T(1,128)} %reshape.285), calls=%async_computation | async-start | bytes 8192 | tf_op jit(solution)/shard_map/all_to_all | solution.py:119
  20.1 4.4 %all-to-all-done = s32[4,1,144]{2,1,0:T(1,128)S(1)} async-done(((s32[4,1,144]{2,1,0:T(1,128)}), s32[4,1,144]{2,1,0:T(1,128)S(1)}, u32[]{:S(2)}, u32[]{:S(2)}) %all-to-all-start) | async-done | bytes 2336 | tf_op jit(solution)/shard_map/all_to_all | solution.py:119
  26.6 5.7 %broadcast_select_fusion = (bf16[3,1024,512]{2,1,0:T(8,128)(2,1)}, bf16[3,1024,512]{2,1,0:T(8,128)(2,1)}) fusion(bf16[3,1024,512]{2,1,0:T(8,128)(2,1)S(1)} %collective-permute-done, pred[]{:T(512)S(6)} %eq.52, bf16[1,4,1024,1024]{3,2,1,0:T(8,128)(2,1)} %param.13, s32[]{:T(128)S(6)} %select_n.144), kind=kLoop, calls=%fused_computation.18 | loop fusion | flops 1572864 | bytes 12582917 | tf_op jit(solution)/shard_map/jit(_where)/select_n | solution.py:41
  32.4 11.2 %gather_fusion.2 = bf16[640,512]{1,0:T(8,128)(2,1)} fusion(bf16[16384,512]{1,0:T(8,128)(2,1)} %param.11, s32[1024]{0:T(1024)S(1)} %pad_clamp_fusion), kind=kCustom, calls=%fused_computation.2 | custom fusion | bytes 1313280 | tf_op jit(solution)/shard_map/jit(_take)/gather | solution.py:130
  55.5 60.0 %collective-permute-done.2 = bf16[3,1024,512]{2,1,0:T(8,128)(2,1)} collective-permute-done((bf16[3,1024,512]{2,1,0:T(8,128)(2,1)}, bf16[3,1024,512]{2,1,0:T(8,128)(2,1)}, u32[]{:S(2)}, u32[]{:S(2)}) %collective-permute-start.2) | collective-permute-done | bytes 3145760 | tf_op jit(solution)/shard_map/ppermute | solution.py:64
  122.3 3.9 %convert_element_type.83 = f32[640,4096]{1,0:T(8,128)S(1)} convert(bf16[640,4096]{1,0:T(8,128)(2,1)} %all-gather.3.cloned.1.call-done) | non-fusion elementwise | flops 2621440 | bytes 15728640 | tf_op jit(solution)/shard_map/convert_element_type | solution.py:134
  130.2 3.9 %fusion.23 = f32[576,3,512]{2,0,1:T(8,128)S(1)} fusion(bf16[3,1024,512]{2,1,0:T(8,128)(2,1)} %get-tuple-element.32, bf16[576,4096]{1,0:T(8,128)(2,1)S(1)} %fusion.4, s32[]{:T(128)S(6)} %select_n.149), kind=kOutput, calls=%fused_computation.42 | convolution fusion | flops 1811939328 | bytes 7864324 | tf_op jit(solution)/shard_map/rn,knh->rkh/dot_general | solution.py:86
  134.1 4.0 %fusion.21 = f32[576,3,512]{2,0,1:T(8,128)S(1)} fusion(bf16[3,1024,512]{2,1,0:T(8,128)(2,1)} %collective-permute-done.1, bf16[576,4096]{1,0:T(8,128)(2,1)S(1)} %fusion.4, s32[]{:T(128)S(6)} %select_n.150), kind=kOutput, calls=%fused_computation.40 | convolution fusion | flops 1811939328 | bytes 7864324 | tf_op jit(solution)/shard_map/rn,knh->rkh/dot_general | solution.py:86
  138.1 4.1 %add_add_fusion = f32[576,3,512]{2,0,1:T(8,128)S(1)} fusion(f32[576,3,512]{2,0,1:T(8,128)S(1)} %fusion.23, f32[576,3,512]{2,0,1:T(8,128)S(1)} %fusion.21, bf16[3,1024,512]{2,1,0:T(8,128)(2,1)} %collective-permute-done.2, bf16[576,4096]{1,0:T(8,128)(2,1)S(1)} %fusion.4, s32[]{:T(128)S(6)} %select_n.151), kind=kOutput, calls=%fused_computation.15 | convolution fusion | flops 1813708800 | bytes 14942212 | tf_op jit(solution)/shard_map/rn,knh->rkh/dot_general | solution.py:86
  146.0 9.8 %collective-permute-done.3 = bf16[3,512,512]{2,1,0:T(8,128)(2,1)} collective-permute-done((bf16[3,512,512]{2,1,0:T(8,128)(2,1)}, bf16[3,512,512]{2,1,0:T(8,128)(2,1)}, u32[]{:S(2)}, u32[]{:S(2)}) %collective-permute-start.3) | collective-permute-done | bytes 1572896 | tf_op jit(solution)/shard_map/ppermute | solution.py:73
  172.9 4.2 %fusion.85 = (f32[12,8,48]{2,1,0:T(8,128)S(1)}, f32[12,8,48,48]{2,3,1,0:T(8,128)S(1)}) fusion(f32[12,8,48,48]{2,3,1,0:T(8,128)S(1)} %fusion.26), kind=kOutput, calls=%fused_computation.142 | output fusion | flops 884783 | bytes 1787904 | tf_op jit(solution)/shard_map/sub | solution.py:20
  196.4 4.3 %convolution_convert_fusion = bf16[576,4096]{1,0:T(8,128)(2,1)} fusion(bf16[576,512]{1,0:T(8,128)(2,1)S(1)} %copy-done.11, bf16[4096,512]{1,0:T(8,128)(2,1)S(1)} %bitcast_dynamic-update-slice_fusion.8), kind=kOutput, calls=%fused_computation.12 | convolution fusion | flops 2418278400 | bytes 9502720 | tf_op jit(solution)/shard_map/dot_general | solution.py:148
  207.5 4.1 %all-to-all-start.1 = ((bf16[64,4,1024]{2,0,1:T(8,128)(2,1)}), bf16[64,4,1024]{2,0,1:T(8,128)(2,1)}, u32[]{:S(2)}, u32[]{:S(2)}) async-start(bf16[64,4,1024]{2,0,1:T(8,128)(2,1)} %bitcast.145), calls=%async_computation.2 | async-start | bytes 1048576 | tf_op jit(solution)/shard_map/all_to_all | solution.py:157
  211.7 38.4 %all-to-all-done.1 = bf16[64,4,1024]{2,0,1:T(8,128)(2,1)} async-done(((bf16[64,4,1024]{2,0,1:T(8,128)(2,1)}), bf16[64,4,1024]{2,0,1:T(8,128)(2,1)}, u32[]{:S(2)}, u32[]{:S(2)}) %all-to-all-start.1) | async-done | bytes 524320 | tf_op jit(solution)/shard_map/all_to_all | solution.py:157
  252.7 3.6 all-to-all-start.2
  256.7 8.7 %all-to-all-done.2 = f32[4,64,512]{2,1,0:T(8,128)S(1)} async-done(((f32[4,64,512]{2,1,0:T(8,128)}), f32[4,64,512]{2,1,0:T(8,128)S(1)}, u32[]{:S(2)}, u32[]{:S(2)}) %all-to-all-start.2) | async-done | bytes 524320 | tf_op jit(solution)/shard_map/all_to_all | solution.py:161
  272.2 14.0 %collective-permute-done.12 = bf16[2,512,512]{2,1,0:T(8,128)(2,1)S(1)} collective-permute-done((bf16[2,512,512]{2,1,0:T(8,128)(2,1)S(1)}, bf16[2,512,512]{2,1,0:T(8,128)(2,1)S(1)}, u32[]{:S(2)}, u32[]{:S(2)}) %collective-permute-start.12) | collective-permute-done | bytes 1048608 | tf_op jit(solution)/shard_map/ppermute | solution.py:73
  296.9 13.1 %collective-permute-done.14 = bf16[1,1024,512]{2,1,0:T(8,128)(2,1)S(1)} collective-permute-done((bf16[1,1024,512]{2,1,0:T(8,128)(2,1)}, bf16[1,1024,512]{2,1,0:T(8,128)(2,1)S(1)}, u32[]{:S(2)}, u32[]{:S(2)}) %collective-permute-start.14) | collective-permute-done | bytes 1048608 | tf_op jit(solution)/shard_map/ppermute | solution.py:63
  312.2 7.9 %all-gather.5.cloned.1.call-done = bf16[576,4096]{1,0:T(8,128)(2,1)} async-done(((bf16[576,512]{1,0:T(8,128)(2,1)}), bf16[576,4096]{1,0:T(8,128)(2,1)}) %all-gather.5.cloned.1.call-update) | async-done | bytes 4718608 | tf_op jit(solution)/shard_map/all_gather | solution.py:166
  320.1 4.3 %fusion.3 = (f32[576]{0:T(1024)S(1)}, bf16[576,4096]{1,0:T(8,128)(2,1)S(1)}) fusion(bf16[576,4096]{1,0:T(8,128)(2,1)} %all-gather.5.cloned.1.call-done, f32[4096]{0:T(1024)S(1)} %bitcast.149), kind=kLoop, calls=%fused_computation.9 | loop fusion | flops 11795904 | bytes 9455872 | tf_op jit(solution)/shard_map/reduce_sum | solution.py:171
  344.6 8.5 %collective-permute-done.16 = bf16[1,512,512]{2,1,0:T(8,128)(2,1)} collective-permute-done((bf16[1,512,512]{2,1,0:T(8,128)(2,1)}, bf16[1,512,512]{2,1,0:T(8,128)(2,1)}, u32[]{:S(2)}, u32[]{:S(2)}) %collective-permute-start.16) | collective-permute-done | bytes 524320 | tf_op jit(solution)/shard_map/ppermute | solution.py:73
  357.0 3.6 convolution_convert_fusion.1
  360.7 17.8 %all_to_all.40 = bf16[64,8,512]{2,0,1:T(8,128)(2,1)S(1)} all-to-all(bf16[64,8,512]{2,0,1:T(8,128)(2,1)S(1)} %bitcast.146), channel_id=1, replica_groups=mesh['shard'=4,'mp'=4,'segment'=2] {'mp','segment'}, dimensions={1} | all-to-all | bytes 1048576 | tf_op jit(solution)/shard_map/all_to_all | solution.py:183
  (174 shorter events, 123.3 us)
Async XLA Ops:
  11.0 15.6 %collective-permute-start = (bf16[3,1024,512]{2,1,0:T(8,128)(2,1)}, bf16[3,1024,512]{2,1,0:T(8,128)(2,1)S(1)}, u32[]{:S(2)}, u32[]{:S(2)}) collective-permute-start(bf16[3,1024,512]{2,1,0:T(8,128)(2,1)} %dynamic-slice_bitcast_fusion), channel_id=1, source_target_pairs={{0,1},{1,0},{2,3},{3,2},{4,5},{5,4},{6,7},{7,6},{8,9},{9,8},{10,11... | collective-permute-start | bytes 9437192 | tf_op jit(solution)/shard_map/ppermute | solution.py:40
  15.2 9.4 %all-to-all-start = ((s32[4,1,144]{2,1,0:T(1,128)}), s32[4,1,144]{2,1,0:T(1,128)S(1)}, u32[]{:S(2)}, u32[]{:S(2)}) async-start(s32[4,1,144]{2,1,0:T(1,128)} %reshape.285), calls=%async_computation | async-start | bytes 8192 | tf_op jit(solution)/shard_map/all_to_all | solution.py:119
  19.9 102.4 %all-gather.3.cloned.1.call-start = ((), (), s32[]{:S(2)}) async-start(), calls=%async_computation.5 | async-start | bytes 5898240 | tf_op jit(solution)/shard_map/all_gather | solution.py:131
  45.8 219.7 %reduce-scatter.2.cloned.1.call-start = ((), (), s32[]{:S(2)}) async-start(), calls=%async_computation.6 | async-start | bytes 5308416 | tf_op jit(solution)/shard_map/reduce_scatter | solution.py:154
  46.0 69.5 %collective-permute-start.2 = (bf16[3,1024,512]{2,1,0:T(8,128)(2,1)}, bf16[3,1024,512]{2,1,0:T(8,128)(2,1)}, u32[]{:S(2)}, u32[]{:S(2)}) collective-permute-start(bf16[3,1024,512]{2,1,0:T(8,128)(2,1)} %get-tuple-element.32), channel_id=1, source_target_pairs={{0,16},{8,24},{16,0},{24,8},{1,17},{9,25},{17,1},{25,9},{2,18},{10... | collective-permute-start | bytes 9437192 | tf_op jit(solution)/shard_map/ppermute | solution.py:64
  46.6 72.2 %collective-permute-start.1 = (bf16[3,1024,512]{2,1,0:T(8,128)(2,1)}, bf16[3,1024,512]{2,1,0:T(8,128)(2,1)}, u32[]{:S(2)}, u32[]{:S(2)}) collective-permute-start(bf16[3,1024,512]{2,1,0:T(8,128)(2,1)} %get-tuple-element.32), channel_id=1, source_target_pairs={{0,8},{8,0},{16,24},{24,16},{1,9},{9,1},{17,25},{25,17},{2,10},{10... | collective-permute-start | bytes 9437192 | tf_op jit(solution)/shard_map/ppermute | solution.py:63
  49.5 3.0 collective-permute-start.5
  118.2 37.6 %collective-permute-start.3 = (bf16[3,512,512]{2,1,0:T(8,128)(2,1)}, bf16[3,512,512]{2,1,0:T(8,128)(2,1)}, u32[]{:S(2)}, u32[]{:S(2)}) collective-permute-start(bf16[3,512,512]{2,1,0:T(8,128)(2,1)} %slice.104), channel_id=1, source_target_pairs={{0,8},{8,0},{16,24},{24,16},{1,9},{9,1},{17,25},{25,17},{2,10},{10... | collective-permute-start | bytes 4718600 | tf_op jit(solution)/shard_map/ppermute | solution.py:73
  121.4 37.6 %collective-permute-start.4 = (bf16[3,512,512]{2,1,0:T(8,128)(2,1)}, bf16[3,512,512]{2,1,0:T(8,128)(2,1)}, u32[]{:S(2)}, u32[]{:S(2)}) collective-permute-start(bf16[3,512,512]{2,1,0:T(8,128)(2,1)} %slice.105), channel_id=1, source_target_pairs={{0,16},{8,24},{16,0},{24,8},{1,17},{9,25},{17,1},{25,9},{2,18},{10... | collective-permute-start | bytes 4718600 | tf_op jit(solution)/shard_map/ppermute | solution.py:74
  142.2 43.8 %collective-permute-start.6 = (bf16[1,1024,512]{2,1,0:T(8,128)(2,1)}, bf16[1,1024,512]{2,1,0:T(8,128)(2,1)}, u32[]{:S(2)}, u32[]{:S(2)}) collective-permute-start(bf16[1,1024,512]{2,1,0:T(8,128)(2,1)} %get-tuple-element.16), channel_id=1, source_target_pairs={{0,8},{8,0},{16,24},{24,16},{1,9},{9,1},{17,25},{25,17},{2,10},{10... | collective-permute-start | bytes 3145736 | tf_op jit(solution)/shard_map/ppermute | solution.py:63
  143.5 39.9 %collective-permute-start.7 = (bf16[1,1024,512]{2,1,0:T(8,128)(2,1)}, bf16[1,1024,512]{2,1,0:T(8,128)(2,1)}, u32[]{:S(2)}, u32[]{:S(2)}) collective-permute-start(bf16[1,1024,512]{2,1,0:T(8,128)(2,1)} %get-tuple-element.16), channel_id=1, source_target_pairs={{0,16},{8,24},{16,0},{24,8},{1,17},{9,25},{17,1},{25,9},{2,18},{10... | collective-permute-start | bytes 3145736 | tf_op jit(solution)/shard_map/ppermute | solution.py:64
  184.5 9.2 %collective-permute-start.8 = (bf16[1,512,512]{2,1,0:T(8,128)(2,1)S(1)}, bf16[1,512,512]{2,1,0:T(8,128)(2,1)S(1)}, u32[]{:S(2)}, u32[]{:S(2)}) collective-permute-start(bf16[1,512,512]{2,1,0:T(8,128)(2,1)S(1)} %slice.109), channel_id=1, source_target_pairs={{0,8},{8,0},{16,24},{24,16},{1,9},{9,1},{17,25},{25,17},{2,10},{10... | collective-permute-start | bytes 1572872 | tf_op jit(solution)/shard_map/ppermute | solution.py:73
  187.1 9.2 %collective-permute-start.9 = (bf16[1,512,512]{2,1,0:T(8,128)(2,1)S(1)}, bf16[1,512,512]{2,1,0:T(8,128)(2,1)S(1)}, u32[]{:S(2)}, u32[]{:S(2)}) collective-permute-start(bf16[1,512,512]{2,1,0:T(8,128)(2,1)S(1)} %slice.110), channel_id=1, source_target_pairs={{0,16},{8,24},{16,0},{24,8},{1,17},{9,25},{17,1},{25,9},{2,18},{10... | collective-permute-start | bytes 1572872 | tf_op jit(solution)/shard_map/ppermute | solution.py:74
  203.9 62.8 %collective-permute-start.10 = (bf16[2,1024,512]{2,1,0:T(8,128)(2,1)}, bf16[2,1024,512]{2,1,0:T(8,128)(2,1)}, u32[]{:S(2)}, u32[]{:S(2)}) collective-permute-start(bf16[2,1024,512]{2,1,0:T(8,128)(2,1)} %slice_select_fusion), channel_id=1, source_target_pairs={{0,8},{8,0},{16,24},{24,16},{1,9},{9,1},{17,25},{25,17},{2,10},{10... | collective-permute-start | bytes 6291464 | tf_op jit(solution)/shard_map/ppermute | solution.py:63
  204.5 62.3 %collective-permute-start.11 = (bf16[2,1024,512]{2,1,0:T(8,128)(2,1)}, bf16[2,1024,512]{2,1,0:T(8,128)(2,1)}, u32[]{:S(2)}, u32[]{:S(2)}) collective-permute-start(bf16[2,1024,512]{2,1,0:T(8,128)(2,1)} %slice_select_fusion), channel_id=1, source_target_pairs={{0,16},{8,24},{16,0},{24,8},{1,17},{9,25},{17,1},{25,9},{2,18},{10... | collective-permute-start | bytes 6291464 | tf_op jit(solution)/shard_map/ppermute | solution.py:64
  207.5 42.5 %all-to-all-start.1 = ((bf16[64,4,1024]{2,0,1:T(8,128)(2,1)}), bf16[64,4,1024]{2,0,1:T(8,128)(2,1)}, u32[]{:S(2)}, u32[]{:S(2)}) async-start(bf16[64,4,1024]{2,0,1:T(8,128)(2,1)} %bitcast.145), calls=%async_computation.2 | async-start | bytes 1048576 | tf_op jit(solution)/shard_map/all_to_all | solution.py:157
  252.7 12.7 %all-to-all-start.2 = ((f32[4,64,512]{2,1,0:T(8,128)}), f32[4,64,512]{2,1,0:T(8,128)S(1)}, u32[]{:S(2)}, u32[]{:S(2)}) async-start(f32[4,64,512]{2,1,0:T(8,128)} %fusion.38), calls=%async_computation.3 | async-start | bytes 1048576 | tf_op jit(solution)/shard_map/all_to_all | solution.py:161
  256.3 63.8 %all-gather.5.cloned.1.call-start = ((), (), s32[]{:S(2)}) async-start(), calls=%async_computation.7 | async-start | bytes 5308416 | tf_op jit(solution)/shard_map/all_gather | solution.py:166
  269.1 17.2 %collective-permute-start.12 = (bf16[2,512,512]{2,1,0:T(8,128)(2,1)S(1)}, bf16[2,512,512]{2,1,0:T(8,128)(2,1)S(1)}, u32[]{:S(2)}, u32[]{:S(2)}) collective-permute-start(bf16[2,512,512]{2,1,0:T(8,128)(2,1)S(1)} %slice.117), channel_id=1, source_target_pairs={{0,8},{8,0},{16,24},{24,16},{1,9},{9,1},{17,25},{25,17},{2,10},{10... | collective-permute-start | bytes 3145736 | tf_op jit(solution)/shard_map/ppermute | solution.py:73
  272.0 16.7 %collective-permute-start.13 = (bf16[2,512,512]{2,1,0:T(8,128)(2,1)S(1)}, bf16[2,512,512]{2,1,0:T(8,128)(2,1)S(1)}, u32[]{:S(2)}, u32[]{:S(2)}) collective-permute-start(bf16[2,512,512]{2,1,0:T(8,128)(2,1)S(1)} %slice.118), channel_id=1, source_target_pairs={{0,16},{8,24},{16,0},{24,8},{1,17},{9,25},{17,1},{25,9},{2,18},{10... | collective-permute-start | bytes 3145736 | tf_op jit(solution)/shard_map/ppermute | solution.py:74
  294.9 15.0 %collective-permute-start.14 = (bf16[1,1024,512]{2,1,0:T(8,128)(2,1)}, bf16[1,1024,512]{2,1,0:T(8,128)(2,1)S(1)}, u32[]{:S(2)}, u32[]{:S(2)}) collective-permute-start(bf16[1,1024,512]{2,1,0:T(8,128)(2,1)} %get-tuple-element.29), channel_id=1, source_target_pairs={{0,8},{8,0},{16,24},{24,16},{1,9},{9,1},{17,25},{25,17},{2,10},{10... | collective-permute-start | bytes 3145736 | tf_op jit(solution)/shard_map/ppermute | solution.py:63
  294.9 16.1 %collective-permute-start.15 = (bf16[1,1024,512]{2,1,0:T(8,128)(2,1)}, bf16[1,1024,512]{2,1,0:T(8,128)(2,1)S(1)}, u32[]{:S(2)}, u32[]{:S(2)}) collective-permute-start(bf16[1,1024,512]{2,1,0:T(8,128)(2,1)} %get-tuple-element.29), channel_id=1, source_target_pairs={{0,16},{8,24},{16,0},{24,8},{1,17},{9,25},{17,1},{25,9},{2,18},{10... | collective-permute-start | bytes 3145736 | tf_op jit(solution)/shard_map/ppermute | solution.py:64
  338.7 14.4 %collective-permute-start.16 = (bf16[1,512,512]{2,1,0:T(8,128)(2,1)}, bf16[1,512,512]{2,1,0:T(8,128)(2,1)}, u32[]{:S(2)}, u32[]{:S(2)}) collective-permute-start(bf16[1,512,512]{2,1,0:T(8,128)(2,1)} %slice.94), channel_id=1, source_target_pairs={{0,8},{8,0},{16,24},{24,16},{1,9},{9,1},{17,25},{25,17},{2,10},{10... | collective-permute-start | bytes 1572872 | tf_op jit(solution)/shard_map/ppermute | solution.py:73
  341.0 14.1 %collective-permute-start.17 = (bf16[1,512,512]{2,1,0:T(8,128)(2,1)}, bf16[1,512,512]{2,1,0:T(8,128)(2,1)}, u32[]{:S(2)}, u32[]{:S(2)}) collective-permute-start(bf16[1,512,512]{2,1,0:T(8,128)(2,1)} %slice.95), channel_id=1, source_target_pairs={{0,16},{8,24},{16,0},{24,8},{1,17},{9,25},{17,1},{25,9},{2,18},{10... | collective-permute-start | bytes 1572872 | tf_op jit(solution)/shard_map/ppermute | solution.py:74
  (19 other events, 155.0 us)
Sparse Core Ops, SparseCore 0:
  45.9 55.3 all-gather.2
  200.9 54.6 reduce-scatter.1
  267.9 52.1 all-gather.4
where the time goes:
time: 387 us; the launch traced here: 386 us
  waiting for transfers between devices  177 us (46%)
  local copies, waits for them, and re-layouts  65.8 us (17%)
  matrix products  43.6 us (11%)
  other arithmetic  38.4 us (10%)
  starting transfers between devices  28.8 us (7%)
  blocking collectives  17.8 us (5%)
  between operations  14.3 us (4%)
    ppermute x4, waiting for transfers between devices, near(): lax.ppermute(block, 'shard', Y_PAIRS)  60 us
    all_to_all x1, waiting for transfers between devices, body(): lax.all_to_all(after(targ_normed, enc_partial), 'shard', split_axis=1, co...  38.4 us
    ppermute x4, waiting for transfers between devices, far(): top = lax.ppermute(pieces[2][2][:, :rows // 2], 'shard', X_PAIRS)  35.6 us
    dot_general x10, matrix products, project(): jnp.einsum('rn,knh->rkh', part, block, preferred_element_type=jnp.float32)  28 us
    all_to_all x1, blocking collectives, body(): lax.all_to_all(dec_partial, ('mp', 'segment'), split_axis=1, concat_axis=...  17.8 us
    ppermute x4, waiting for transfers between devices, near(): lax.ppermute(block, 'shard', X_PAIRS)  13.1 us
    gather x1, local copies, waits for them, and re-layouts, body(): embedded_part = jnp.take(vocab_table, all_ids, axis=0)  11.2 us
    dynamic_update_slice x9, local copies, waits for them, and re-layouts, in_order(): lax.dynamic_update_slice_in_dim(whole, block[0], owner * shard_rows + fir...  10.2 us
  transfers between devices with their start and end apart: 24, of which 15 were waited for; matrix products, arithmetic and copies ran while one was open for 24% of the time, Pallas kernels for 0%

commit v1 on v0

--- a/solution.py
+++ b/solution.py
@@ -6,6 +6,19 @@
 D = 4096
 DH = 64
 epsilon = 1e-06
+
+
+def ring_gather(x, axis, dim):
+    ways = lax.axis_size(axis)
+    up = [(d, (d + 1) % ways) for d in range(ways)]
+    down = [(d, (d - 1) % ways) for d in range(ways)]
+    earlier, later = ([x], [x])
+    for _ in range(ways // 2):
+        earlier.append(lax.ppermute(earlier[-1], axis, up))
+    for _ in range((ways - 1) // 2):
+        later.append(lax.ppermute(later[-1], axis, down))
+    line = jnp.concatenate([*earlier[::-1], *later[1:]], axis=dim)
+    return jnp.roll(line, (lax.axis_index(axis) - ways // 2) * x.shape[dim], axis=dim)
 
 
 def attend(query_rows, key_rows, value_rows, head_count):
@@ -163,7 +176,7 @@
     queries = (targ_accum * scale[pass_rows:, None]).astype(jnp.bfloat16)[None]
     enc_sum = after(enc_sum, queries, *blocks(cross_near))
     encoded = (passage_part.astype(jnp.float32) + enc_sum).astype(jnp.bfloat16)
-    whole_encoded = lax.all_gather(encoded, ("mp", "segment"), axis=1, tiled=True)
+    whole_encoded = ring_gather(encoded, ("mp", "segment"), 1)
     cross_far = far(cross_near)
     late_near = near(dec_out(*blocks(cross_far), queries))
     whole_encoded = after(whole_encoded, *blocks(cross_far))

time: 387 us -> 407 us (1.052); the launches traced: 386 us -> 401 us
  starting transfers between devices: 28.8 us -> 37.1 us
  local copies, waits for them, and re-layouts: 65.8 us -> 74 us
    ppermute x0 -> x7, waiting for transfers between devices: none -> 27.9 us  [the longest x3 14.8 us: ring_gather(): later.append(lax.ppermute(later[-1], axis, down))]
    ppermute x4, waiting for transfers between devices: 35.6 us -> 19 us  [far(): top = lax.ppermute(pieces[2][2][:, :rows // 2], 'shard', X_PAIRS)]
    ppermute x4, waiting for transfers between devices: 13.1 us -> 2.15 us  [near(): lax.ppermute(block, 'shard', X_PAIRS)]
    ppermute x0 -> x7, starting transfers between devices: none -> 8.18 us  [the longest x3 8.11 us: ring_gather(): later.append(lax.ppermute(later[-1], axis, down))]
    all_gather x1 -> x0, waiting for transfers between devices: 7.94 us -> none  [body(): lax.all_gather(encoded, ('mp', 'segment'), axis=1, tiled=True)]
    unnamed x42 -> x51, local copies, waits for them, and re-layouts: 5.32 us -> 11.8 us
    ppermute x4, waiting for transfers between devices: 60 us -> 64.6 us  [near(): lax.ppermute(block, 'shard', Y_PAIRS)]
  transfers between devices with their start and end apart: 24 -> 30, of which waited for: 15 -> 19; matrix products, arithmetic and copies ran while one was open for 24% -> 24% of each run, Pallas kernels for 0% -> 0%
where the time goes in v1:
time: 407 us; the launch traced here: 401 us
  waiting for transfers between devices  174 us (43%)
  local copies, waits for them, and re-layouts  74 us (18%)
  matrix products  45.9 us (11%)
  starting transfers between devices  37.1 us (9%)
  other arithmetic  36.1 us (9%)
  blocking collectives  18.7 us (5%)
  between operations  14.9 us (4%)
    ppermute x4, waiting for transfers between devices, near(): lax.ppermute(block, 'shard', Y_PAIRS)  64.6 us
    all_to_all x1, waiting for transfers between devices, body(): lax.all_to_all(after(targ_normed, enc_partial), 'shard', split_axis=1, co...  38.7 us
    dot_general x10, matrix products, project(): jnp.einsum('rn,knh->rkh', part, block, preferred_element_type=jnp.float32)  30.3 us
    ppermute x4, waiting for transfers between devices, far(): top = lax.ppermute(pieces[2][2][:, :rows // 2], 'shard', X_PAIRS)  19 us
    all_to_all x1, blocking collectives, body(): lax.all_to_all(dec_partial, ('mp', 'segment'), split_axis=1, concat_axis=...  18.7 us
    ppermute x3, waiting for transfers between devices, ring_gather(): later.append(lax.ppermute(later[-1], axis, down))  14.8 us
    ppermute x4, waiting for transfers between devices, ring_gather(): earlier.append(lax.ppermute(earlier[-1], axis, up))  13.1 us
    unnamed x51, local copies, waits for them, and re-layouts  11.8 us
  transfers between devices with their start and end apart: 30, of which 19 were waited for; matrix products, arithmetic and copies ran while one was open for 24% of the time, Pallas kernels for 0%

profile of v1, /device:TPU:0, one launch (start us, length us, event | category | flops | bytes accessed | tf_op | source)
XLA Modules:
  0.0 401.0 jit_solution(2733511909708295567)
XLA Ops:
  7.2 3.8 dynamic-slice_bitcast_fusion
  15.1 4.7 %all-to-all-start = ((s32[4,1,144]{2,1,0:T(1,128)}), s32[4,1,144]{2,1,0:T(1,128)S(1)}, u32[]{:S(2)}, u32[]{:S(2)}) async-start(s32[4,1,144]{2,1,0:T(1,128)} %reshape.285), calls=%async_computation | async-start | bytes 8192 | tf_op jit(solution)/shard_map/all_to_all | solution.py:132
  20.1 4.4 %all-to-all-done = s32[4,1,144]{2,1,0:T(1,128)S(1)} async-done(((s32[4,1,144]{2,1,0:T(1,128)}), s32[4,1,144]{2,1,0:T(1,128)S(1)}, u32[]{:S(2)}, u32[]{:S(2)}) %all-to-all-start) | async-done | bytes 2336 | tf_op jit(solution)/shard_map/all_to_all | solution.py:132
  26.6 5.7 %broadcast_select_fusion = (bf16[3,1024,512]{2,1,0:T(8,128)(2,1)}, bf16[3,1024,512]{2,1,0:T(8,128)(2,1)}) fusion(bf16[3,1024,512]{2,1,0:T(8,128)(2,1)S(1)} %collective-permute-done, pred[]{:T(512)S(6)} %eq.55, bf16[1,4,1024,1024]{3,2,1,0:T(8,128)(2,1)} %param.13, s32[]{:T(128)S(6)} %select_n.157), kind=kLoop, calls=%fused_computation.18 | loop fusion | flops 1572864 | bytes 12582917 | tf_op jit(solution)/shard_map/jit(_where)/select_n | solution.py:54
  32.3 11.3 %gather_fusion.2 = bf16[640,512]{1,0:T(8,128)(2,1)} fusion(bf16[16384,512]{1,0:T(8,128)(2,1)} %param.11, s32[1024]{0:T(1024)S(1)} %pad_clamp_fusion), kind=kCustom, calls=%fused_computation.2 | custom fusion | bytes 1313280 | tf_op jit(solution)/shard_map/jit(_take)/gather | solution.py:143
  55.7 60.0 %collective-permute-done.2 = bf16[3,1024,512]{2,1,0:T(8,128)(2,1)} collective-permute-done((bf16[3,1024,512]{2,1,0:T(8,128)(2,1)}, bf16[3,1024,512]{2,1,0:T(8,128)(2,1)}, u32[]{:S(2)}, u32[]{:S(2)}) %collective-permute-start.2) | collective-permute-done | bytes 3145760 | tf_op jit(solution)/shard_map/ppermute | solution.py:77
  122.5 3.9 convert_element_type.83
  130.4 3.9 fusion.23
  134.3 4.0 %fusion.21 = f32[576,3,512]{2,0,1:T(8,128)S(1)} fusion(bf16[3,1024,512]{2,1,0:T(8,128)(2,1)} %collective-permute-done.1, bf16[576,4096]{1,0:T(8,128)(2,1)S(1)} %fusion.4, s32[]{:T(128)S(6)} %select_n.163), kind=kOutput, calls=%fused_computation.40 | convolution fusion | flops 1811939328 | bytes 7864324 | tf_op jit(solution)/shard_map/rn,knh->rkh/dot_general | solution.py:99
  138.4 4.1 %add_add_fusion = f32[576,3,512]{2,0,1:T(8,128)S(1)} fusion(f32[576,3,512]{2,0,1:T(8,128)S(1)} %fusion.23, f32[576,3,512]{2,0,1:T(8,128)S(1)} %fusion.21, bf16[3,1024,512]{2,1,0:T(8,128)(2,1)} %collective-permute-done.2, bf16[576,4096]{1,0:T(8,128)(2,1)S(1)} %fusion.4, s32[]{:T(128)S(6)} %select_n.164), kind=kOutput, calls=%fused_computation.15 | convolution fusion | flops 1813708800 | bytes 14942212 | tf_op jit(solution)/shard_map/rn,knh->rkh/dot_general | solution.py:99
  146.3 9.8 %collective-permute-done.3 = bf16[3,512,512]{2,1,0:T(8,128)(2,1)} collective-permute-done((bf16[3,512,512]{2,1,0:T(8,128)(2,1)}, bf16[3,512,512]{2,1,0:T(8,128)(2,1)}, u32[]{:S(2)}, u32[]{:S(2)}) %collective-permute-start.3) | collective-permute-done | bytes 1572896 | tf_op jit(solution)/shard_map/ppermute | solution.py:86
  173.3 4.2 %fusion.85 = (f32[12,8,48]{2,1,0:T(8,128)S(1)}, f32[12,8,48,48]{2,3,1,0:T(8,128)S(1)}) fusion(f32[12,8,48,48]{2,3,1,0:T(8,128)S(1)} %fusion.26), kind=kOutput, calls=%fused_computation.159 | output fusion | flops 884783 | bytes 1787904 | tf_op jit(solution)/shard_map/sub | solution.py:33
  196.8 4.4 %convolution_convert_fusion = bf16[576,4096]{1,0:T(8,128)(2,1)} fusion(bf16[576,512]{1,0:T(8,128)(2,1)S(1)} %copy-done.7, bf16[4096,512]{1,0:T(8,128)(2,1)S(1)} %bitcast_dynamic-update-slice_fusion.8), kind=kOutput, calls=%fused_computation.12 | convolution fusion | flops 2418278400 | bytes 9502720 | tf_op jit(solution)/shard_map/dot_general | solution.py:161
  208.0 4.2 %all-to-all-start.1 = ((bf16[64,4,1024]{2,0,1:T(8,128)(2,1)}), bf16[64,4,1024]{2,0,1:T(8,128)(2,1)}, u32[]{:S(2)}, u32[]{:S(2)}) async-start(bf16[64,4,1024]{2,0,1:T(8,128)(2,1)} %bitcast.145), calls=%async_computation.2 | async-start | bytes 1048576 | tf_op jit(solution)/shard_map/all_to_all | solution.py:170
  212.2 38.7 %all-to-all-done.1 = bf16[64,4,1024]{2,0,1:T(8,128)(2,1)} async-done(((bf16[64,4,1024]{2,0,1:T(8,128)(2,1)}), bf16[64,4,1024]{2,0,1:T(8,128)(2,1)}, u32[]{:S(2)}, u32[]{:S(2)}) %all-to-all-start.1) | async-done | bytes 524320 | tf_op jit(solution)/shard_map/all_to_all | solution.py:170
  253.5 3.7 all-to-all-start.2
  257.8 8.9 %all-to-all-done.2 = f32[4,64,512]{2,1,0:T(8,128)S(1)} async-done(((f32[4,64,512]{2,1,0:T(8,128)}), f32[4,64,512]{2,1,0:T(8,128)S(1)}, u32[]{:S(2)}, u32[]{:S(2)}) %all-to-all-start.2) | async-done | bytes 524320 | tf_op jit(solution)/shard_map/all_to_all | solution.py:174
  272.4 11.1 %collective-permute-done.12 = bf16[576,512]{1,0:T(8,128)(2,1)S(1)} collective-permute-done((bf16[576,512]{1,0:T(8,128)(2,1)S(1)}, bf16[576,512]{1,0:T(8,128)(2,1)S(1)}, u32[]{:S(2)}, u32[]{:S(2)}) %collective-permute-start.12) | collective-permute-done | bytes 589856 | tf_op jit(solution)/shard_map/ppermute | solution.py:17
  297.6 8.5 %collective-permute-done.16 = bf16[576,512]{1,0:T(8,128)(2,1)} collective-permute-done((bf16[576,512]{1,0:T(8,128)(2,1)S(1)}, bf16[576,512]{1,0:T(8,128)(2,1)}, u32[]{:S(2)}, u32[]{:S(2)}) %collective-permute-start.16) | collective-permute-done | bytes 589856 | tf_op jit(solution)/shard_map/ppermute | solution.py:19
  306.1 3.8 collective-permute-start.17
  314.2 4.6 %collective-permute-done.22 = bf16[1,1024,512]{2,1,0:T(8,128)(2,1)S(1)} collective-permute-done((bf16[1,1024,512]{2,1,0:T(8,128)(2,1)}, bf16[1,1024,512]{2,1,0:T(8,128)(2,1)S(1)}, u32[]{:S(2)}, u32[]{:S(2)}) %collective-permute-start.22) | collective-permute-done | bytes 1048608 | tf_op jit(solution)/shard_map/ppermute | solution.py:77
  322.5 3.9 collective-permute-start.18
  361.8 5.3 %collective-permute-done.23 = bf16[1,512,512]{2,1,0:T(8,128)(2,1)} collective-permute-done((bf16[1,512,512]{2,1,0:T(8,128)(2,1)}, bf16[1,512,512]{2,1,0:T(8,128)(2,1)}, u32[]{:S(2)}, u32[]{:S(2)}) %collective-permute-start.23) | collective-permute-done | bytes 524320 | tf_op jit(solution)/shard_map/ppermute | solution.py:86
  374.5 18.7 %all_to_all.40 = bf16[64,8,512]{2,0,1:T(8,128)(2,1)S(1)} all-to-all(bf16[64,8,512]{2,0,1:T(8,128)(2,1)S(1)} %bitcast.146), channel_id=1, replica_groups=mesh['shard'=4,'mp'=4,'segment'=2] {'mp','segment'}, dimensions={1} | all-to-all | bytes 1048576 | tf_op jit(solution)/shard_map/all_to_all | solution.py:196
  (196 shorter events, 150.6 us)
Async XLA Ops:
  11.0 15.6 %collective-permute-start = (bf16[3,1024,512]{2,1,0:T(8,128)(2,1)}, bf16[3,1024,512]{2,1,0:T(8,128)(2,1)S(1)}, u32[]{:S(2)}, u32[]{:S(2)}) collective-permute-start(bf16[3,1024,512]{2,1,0:T(8,128)(2,1)} %dynamic-slice_bitcast_fusion), channel_id=1, source_target_pairs={{0,1},{1,0},{2,3},{3,2},{4,5},{5,4},{6,7},{7,6},{8,9},{9,8},{10,11... | collective-permute-start | bytes 9437192 | tf_op jit(solution)/shard_map/ppermute | solution.py:53
  19.9 102.6 %all-gather.2.cloned.1.call-start = ((), (), s32[]{:S(2)}) async-start(), calls=%async_computation.5 | async-start | bytes 5898240 | tf_op jit(solution)/shard_map/all_gather | solution.py:144
  45.7 225.2 %reduce-scatter.2.cloned.1.call-start = ((), (), s32[]{:S(2)}) async-start(), calls=%async_computation.6 | async-start | bytes 5308416 | tf_op jit(solution)/shard_map/reduce_scatter | solution.py:167
  46.2 69.5 %collective-permute-start.2 = (bf16[3,1024,512]{2,1,0:T(8,128)(2,1)}, bf16[3,1024,512]{2,1,0:T(8,128)(2,1)}, u32[]{:S(2)}, u32[]{:S(2)}) collective-permute-start(bf16[3,1024,512]{2,1,0:T(8,128)(2,1)} %get-tuple-element.32), channel_id=1, source_target_pairs={{0,16},{8,24},{16,0},{24,8},{1,17},{9,25},{17,1},{25,9},{2,18},{10... | collective-permute-start | bytes 9437192 | tf_op jit(solution)/shard_map/ppermute | solution.py:77
  46.8 72.2 %collective-permute-start.1 = (bf16[3,1024,512]{2,1,0:T(8,128)(2,1)}, bf16[3,1024,512]{2,1,0:T(8,128)(2,1)}, u32[]{:S(2)}, u32[]{:S(2)}) collective-permute-start(bf16[3,1024,512]{2,1,0:T(8,128)(2,1)} %get-tuple-element.32), channel_id=1, source_target_pairs={{0,8},{8,0},{16,24},{24,16},{1,9},{9,1},{17,25},{25,17},{2,10},{10... | collective-permute-start | bytes 9437192 | tf_op jit(solution)/shard_map/ppermute | solution.py:76
  118.4 37.6 %collective-permute-start.3 = (bf16[3,512,512]{2,1,0:T(8,128)(2,1)}, bf16[3,512,512]{2,1,0:T(8,128)(2,1)}, u32[]{:S(2)}, u32[]{:S(2)}) collective-permute-start(bf16[3,512,512]{2,1,0:T(8,128)(2,1)} %slice.104), channel_id=1, source_target_pairs={{0,8},{8,0},{16,24},{24,16},{1,9},{9,1},{17,25},{25,17},{2,10},{10... | collective-permute-start | bytes 4718600 | tf_op jit(solution)/shard_map/ppermute | solution.py:86
  121.7 37.6 %collective-permute-start.4 = (bf16[3,512,512]{2,1,0:T(8,128)(2,1)}, bf16[3,512,512]{2,1,0:T(8,128)(2,1)}, u32[]{:S(2)}, u32[]{:S(2)}) collective-permute-start(bf16[3,512,512]{2,1,0:T(8,128)(2,1)} %slice.105), channel_id=1, source_target_pairs={{0,16},{8,24},{16,0},{24,8},{1,17},{9,25},{17,1},{25,9},{2,18},{10... | collective-permute-start | bytes 4718600 | tf_op jit(solution)/shard_map/ppermute | solution.py:87
  142.5 43.9 %collective-permute-start.6 = (bf16[1,1024,512]{2,1,0:T(8,128)(2,1)}, bf16[1,1024,512]{2,1,0:T(8,128)(2,1)}, u32[]{:S(2)}, u32[]{:S(2)}) collective-permute-start(bf16[1,1024,512]{2,1,0:T(8,128)(2,1)} %get-tuple-element.16), channel_id=1, source_target_pairs={{0,8},{8,0},{16,24},{24,16},{1,9},{9,1},{17,25},{25,17},{2,10},{10... | collective-permute-start | bytes 3145736 | tf_op jit(solution)/shard_map/ppermute | solution.py:76
  143.7 40.1 %collective-permute-start.7 = (bf16[1,1024,512]{2,1,0:T(8,128)(2,1)}, bf16[1,1024,512]{2,1,0:T(8,128)(2,1)}, u32[]{:S(2)}, u32[]{:S(2)}) collective-permute-start(bf16[1,1024,512]{2,1,0:T(8,128)(2,1)} %get-tuple-element.16), channel_id=1, source_target_pairs={{0,16},{8,24},{16,0},{24,8},{1,17},{9,25},{17,1},{25,9},{2,18},{10... | collective-permute-start | bytes 3145736 | tf_op jit(solution)/shard_map/ppermute | solution.py:77
  204.3 62.3 %collective-permute-start.11 = (bf16[2,1024,512]{2,1,0:T(8,128)(2,1)}, bf16[2,1024,512]{2,1,0:T(8,128)(2,1)}, u32[]{:S(2)}, u32[]{:S(2)}) collective-permute-start(bf16[2,1024,512]{2,1,0:T(8,128)(2,1)} %slice_select_fusion), channel_id=1, source_target_pairs={{0,16},{8,24},{16,0},{24,8},{1,17},{9,25},{17,1},{25,9},{2,18},{10... | collective-permute-start | bytes 6291464 | tf_op jit(solution)/shard_map/ppermute | solution.py:77
  204.9 64.6 %collective-permute-start.10 = (bf16[2,1024,512]{2,1,0:T(8,128)(2,1)}, bf16[2,1024,512]{2,1,0:T(8,128)(2,1)}, u32[]{:S(2)}, u32[]{:S(2)}) collective-permute-start(bf16[2,1024,512]{2,1,0:T(8,128)(2,1)} %slice_select_fusion), channel_id=1, source_target_pairs={{0,8},{8,0},{16,24},{24,16},{1,9},{9,1},{17,25},{25,17},{2,10},{10... | collective-permute-start | bytes 6291464 | tf_op jit(solution)/shard_map/ppermute | solution.py:76
  208.0 42.8 %all-to-all-start.1 = ((bf16[64,4,1024]{2,0,1:T(8,128)(2,1)}), bf16[64,4,1024]{2,0,1:T(8,128)(2,1)}, u32[]{:S(2)}, u32[]{:S(2)}) async-start(bf16[64,4,1024]{2,0,1:T(8,128)(2,1)} %bitcast.145), calls=%async_computation.2 | async-start | bytes 1048576 | tf_op jit(solution)/shard_map/all_to_all | solution.py:170
  253.5 13.2 %all-to-all-start.2 = ((f32[4,64,512]{2,1,0:T(8,128)}), f32[4,64,512]{2,1,0:T(8,128)S(1)}, u32[]{:S(2)}, u32[]{:S(2)}) async-start(f32[4,64,512]{2,1,0:T(8,128)} %fusion.38), calls=%async_computation.3 | async-start | bytes 1048576 | tf_op jit(solution)/shard_map/all_to_all | solution.py:174
  268.0 16.1 %collective-permute-start.19 = (bf16[2,512,512]{2,1,0:T(8,128)(2,1)S(1)}, bf16[2,512,512]{2,1,0:T(8,128)(2,1)}, u32[]{:S(2)}, u32[]{:S(2)}) collective-permute-start(bf16[2,512,512]{2,1,0:T(8,128)(2,1)S(1)} %slice.117), channel_id=1, source_target_pairs={{0,8},{8,0},{16,24},{24,16},{1,9},{9,1},{17,25},{25,17},{2,10},{10... | collective-permute-start | bytes 3145736 | tf_op jit(solution)/shard_map/ppermute | solution.py:86
  270.8 15.5 %collective-permute-start.20 = (bf16[2,512,512]{2,1,0:T(8,128)(2,1)S(1)}, bf16[2,512,512]{2,1,0:T(8,128)(2,1)}, u32[]{:S(2)}, u32[]{:S(2)}) collective-permute-start(bf16[2,512,512]{2,1,0:T(8,128)(2,1)S(1)} %slice.118), channel_id=1, source_target_pairs={{0,16},{8,24},{16,0},{24,8},{1,17},{9,25},{17,1},{25,9},{2,18},{10... | collective-permute-start | bytes 3145736 | tf_op jit(solution)/shard_map/ppermute | solution.py:87
  272.4 11.2 %collective-permute-start.12 = (bf16[576,512]{1,0:T(8,128)(2,1)S(1)}, bf16[576,512]{1,0:T(8,128)(2,1)S(1)}, u32[]{:S(2)}, u32[]{:S(2)}) collective-permute-start(bf16[576,512]{1,0:T(8,128)(2,1)S(1)} %add_convert_fusion), channel_id=1, source_target_pairs={{0,1},{1,2},{2,3},{3,4},{4,5},{5,6},{6,7},{7,0},{8,9},{9,10},{10,1... | collective-permute-start | bytes 1769480 | tf_op jit(solution)/shard_map/ppermute | solution.py:17
  283.5 11.2 %collective-permute-start.13 = (bf16[576,512]{1,0:T(8,128)(2,1)S(1)}, bf16[576,512]{1,0:T(8,128)(2,1)}, u32[]{:S(2)}, u32[]{:S(2)}) collective-permute-start(bf16[576,512]{1,0:T(8,128)(2,1)S(1)} %collective-permute-done.12), channel_id=1, source_target_pairs={{0,1},{1,2},{2,3},{3,4},{4,5},{5,6},{6,7},{7,0},{8,9},{9,10},{10,1... | collective-permute-start | bytes 1769480 | tf_op jit(solution)/shard_map/ppermute | solution.py:17
  291.5 21.7 %collective-permute-start.21 = (bf16[1,1024,512]{2,1,0:T(8,128)(2,1)}, bf16[1,1024,512]{2,1,0:T(8,128)(2,1)S(1)}, u32[]{:S(2)}, u32[]{:S(2)}) collective-permute-start(bf16[1,1024,512]{2,1,0:T(8,128)(2,1)} %get-tuple-element.29), channel_id=1, source_target_pairs={{0,8},{8,0},{16,24},{24,16},{1,9},{9,1},{17,25},{25,17},{2,10},{10... | collective-permute-start | bytes 3145736 | tf_op jit(solution)/shard_map/ppermute | solution.py:76
  292.3 13.8 %collective-permute-start.16 = (bf16[576,512]{1,0:T(8,128)(2,1)S(1)}, bf16[576,512]{1,0:T(8,128)(2,1)}, u32[]{:S(2)}, u32[]{:S(2)}) collective-permute-start(bf16[576,512]{1,0:T(8,128)(2,1)S(1)} %add_convert_fusion), channel_id=1, source_target_pairs={{0,7},{1,0},{2,1},{3,2},{4,3},{5,4},{6,5},{7,6},{8,15},{9,8},{10,9... | collective-permute-start | bytes 1769480 | tf_op jit(solution)/shard_map/ppermute | solution.py:19
  294.7 15.2 %collective-permute-start.14 = (bf16[576,512]{1,0:T(8,128)(2,1)}, bf16[576,512]{1,0:T(8,128)(2,1)}, u32[]{:S(2)}, u32[]{:S(2)}) collective-permute-start(bf16[576,512]{1,0:T(8,128)(2,1)} %collective-permute-done.13), channel_id=1, source_target_pairs={{0,1},{1,2},{2,3},{3,4},{4,5},{5,6},{6,7},{7,0},{8,9},{9,10},{10,1... | collective-permute-start | bytes 1769480 | tf_op jit(solution)/shard_map/ppermute | solution.py:17
  294.7 24.0 %collective-permute-start.22 = (bf16[1,1024,512]{2,1,0:T(8,128)(2,1)}, bf16[1,1024,512]{2,1,0:T(8,128)(2,1)S(1)}, u32[]{:S(2)}, u32[]{:S(2)}) collective-permute-start(bf16[1,1024,512]{2,1,0:T(8,128)(2,1)} %get-tuple-element.29), channel_id=1, source_target_pairs={{0,16},{8,24},{16,0},{24,8},{1,17},{9,25},{17,1},{25,9},{2,18},{10... | collective-permute-start | bytes 3145736 | tf_op jit(solution)/shard_map/ppermute | solution.py:77
  306.1 16.4 %collective-permute-start.17 = (bf16[576,512]{1,0:T(8,128)(2,1)}, bf16[576,512]{1,0:T(8,128)(2,1)S(1)}, u32[]{:S(2)}, u32[]{:S(2)}) collective-permute-start(bf16[576,512]{1,0:T(8,128)(2,1)} %collective-permute-done.16), channel_id=1, source_target_pairs={{0,7},{1,0},{2,1},{3,2},{4,3},{5,4},{6,5},{7,6},{8,15},{9,8},{10,9... | collective-permute-start | bytes 1769480 | tf_op jit(solution)/shard_map/ppermute | solution.py:19
  309.9 16.4 %collective-permute-start.15 = (bf16[576,512]{1,0:T(8,128)(2,1)}, bf16[576,512]{1,0:T(8,128)(2,1)S(1)}, u32[]{:S(2)}, u32[]{:S(2)}) collective-permute-start(bf16[576,512]{1,0:T(8,128)(2,1)} %collective-permute-done.14), channel_id=1, source_target_pairs={{0,1},{1,2},{2,3},{3,4},{4,5},{5,6},{6,7},{7,0},{8,9},{9,10},{10,1... | collective-permute-start | bytes 1769480 | tf_op jit(solution)/shard_map/ppermute | solution.py:17
  322.5 11.3 %collective-permute-start.18 = (bf16[576,512]{1,0:T(8,128)(2,1)S(1)}, bf16[576,512]{1,0:T(8,128)(2,1)S(1)}, u32[]{:S(2)}, u32[]{:S(2)}) collective-permute-start(bf16[576,512]{1,0:T(8,128)(2,1)S(1)} %collective-permute-done.17), channel_id=1, source_target_pairs={{0,7},{1,0},{2,1},{3,2},{4,3},{5,4},{6,5},{7,6},{8,15},{9,8},{10,9... | collective-permute-start | bytes 1769480 | tf_op jit(solution)/shard_map/ppermute | solution.py:19
  (22 other events, 283.2 us)
Sparse Core Ops, SparseCore 0:
  45.8 55.3 all-gather.1
  201.3 54.6 reduce-scatter.1
